TPU v7x, 32 devices: a whole 2x2x4 slice. The times are simulated.
32 devices in a mesh: dp: 8 (over z, y), sp: 4 (over x, core).
Axes of the slice: x: 2, y: 2, z: 4, core: 2. Of those that a mesh axis runs over, the one named last changes fastest.
Arguments:
- tokens: bfloat16 [32, 512, 768], P('dp', 'sp'), may hold values from -6 to 6
- output_grad: bfloat16 [32, 512, 768], P('dp', 'sp'), may hold values from -6 to 6
- segment_ids: int32 [32, 512], P('dp'), may hold values from 0 to 7, as said below
- lengths: int32 [32, 8], P('dp'), may hold values from 1 to 128, as said below
- owner_slot: int32 [48], replicated, may hold values from 0 to 47, as said below
- slot_weights: float32 [48, 384, 384], P('dp')
- first_moment: float32 [48, 384, 384], P('dp'), may hold values from -224 to 224
- second_moment: float32 [48, 384, 384], P('dp'), may hold values from 819.2 to 13107.2
- left_stats: float32 [48, 384, 384], P('dp'), as said below
- right_stats: float32 [48, 384, 384], P('dp'), as said below
- left_basis: float32 [48, 384, 384], P('dp'), as said below
- right_basis: float32 [48, 384, 384], P('dp'), as said below
- vector_values: float32 [3072], P('dp')
- vector_first: float32 [3072], P('dp'), may hold values from -768 to 768
- vector_second: float32 [3072], P('dp'), may hold values from 8192 to 131072
Outputs:
- block_out: bfloat16 [32, 512, 768], P('dp', 'sp')
- input_grad: float32 [32, 512, 768], P('dp', 'sp')
- moment_one: float32 [48, 384, 384], P('dp')
- moment_two: float32 [48, 384, 384], P('dp')
- left_new: float32 [48, 384, 384], P('dp')
- right_new: float32 [48, 384, 384], P('dp')
- weights_new: float32 [48, 384, 384], P('dp')
- weights_half: bfloat16 [48, 384, 384], P('dp')
- vector_one: float32 [3072], P('dp')
- vector_two: float32 [3072], P('dp')
- vector_new: float32 [3072], P('dp')
Inputs may be any that keep to these rules, and one draw needn't show every extreme that they name: `segment_ids`: token t of a row carries passage p iff the sum of that row's first p lengths is at most t and the sum of its first p + 1 lengths is over t. Each row's lengths sum to 512; one length of every row is exactly 128. distinct; block b lies at place owner_slot[b] % 6 of index owner_slot[b] // 6 of dp; some index holds 6 blocks. `left_stats`: each block symmetric and positive definite. `right_stats`: each block symmetric and positive definite. `left_basis`: each block orthogonal. `right_basis`: each block orthogonal.
All inputs are finite; a program needn't handle non-finite values.
Results may differ from a plain program's by a relative error of at most 0.017.
Values may be sent and summed in bfloat16 or wider, within the bound.
A program may use at most 256 MiB of HBM per device.

v0:
```python
import math

import jax
import jax.numpy as jnp
from jax import lax
from jax.experimental import pallas as pl
from jax.experimental.pallas import tpu as pltpu
from jax.sharding import PartitionSpec as P

D = 768
HD = 64
FF = 3072
BLK = 384
STEP = 4


highest = lax.Precision.HIGHEST
rate_matrix = 0.04
rate_vector = 0.2


def layer_norm(summed, gain, shift):
    centre = jnp.mean(summed, axis=-1, keepdims=True)
    centred = summed - centre
    spread = jnp.mean(centred * centred, axis=-1, keepdims=True)
    return centred * lax.rsqrt(spread + 1e-06) * gain + shift


def exact_gelu(values):
    return jax.nn.gelu(values, approximate=False)


def passage_mask(segment_row, length_row):
    starts = jnp.cumsum(length_row) - length_row
    number = length_row.shape[0]
    onehot = (segment_row[:, None] == jnp.arange(number, dtype=jnp.int32)[None, :]).astype(
        jnp.int32
    )
    opening = jnp.sum(onehot * starts[None, :], axis=1)
    closing = opening + jnp.sum(onehot * length_row[None, :], axis=1)
    places = jnp.arange(segment_row.shape[0], dtype=jnp.int32)
    return (places[None, :] >= opening[:, None]) & (places[None, :] < closing[:, None])


def into_blocks(matrix):
    height, breadth = matrix.shape
    return (
        matrix.reshape(height // BLK, BLK, breadth // BLK, BLK)
        .transpose(0, 2, 1, 3)
        .reshape(-1, BLK, BLK)
    )


def from_blocks(blocks, height, breadth):
    return (
        blocks.reshape(height // BLK, breadth // BLK, BLK, BLK)
        .transpose(0, 2, 1, 3)
        .reshape(height, breadth)
    )


def split_blocks(blocks):
    square = (D // BLK) ** 2
    broad = D * FF // (BLK * BLK)
    w_query = from_blocks(blocks[0:square], D, D)
    w_key = from_blocks(blocks[square : 2 * square], D, D)
    w_value = from_blocks(blocks[2 * square : 3 * square], D, D)
    w_output = from_blocks(blocks[3 * square : 4 * square], D, D)
    w_upward = from_blocks(blocks[4 * square : 4 * square + broad], D, FF)
    w_downward = from_blocks(blocks[4 * square + broad : 4 * square + 2 * broad], FF, D)
    return (w_query, w_key, w_value, w_output, w_upward, w_downward)


def contract_rows(left_mat, right_mat):
    return lax.dot_general(
        left_mat, right_mat, (((0,), (0,)), ((), ())), preferred_element_type=jnp.float32
    )


def contract_cols(left_mat, right_mat):
    return lax.dot_general(
        left_mat, right_mat, (((1,), (1,)), ((), ())), preferred_element_type=jnp.float32
    )


def soap_update(
    gradient, weights, moment_old, second_old, left_old, right_old, left_rot, right_rot
):
    left_next = 0.95 * left_old + 0.05 * jnp.einsum(
        "nij,nkj->nik", gradient, gradient, precision=highest
    )
    right_next = 0.95 * right_old + 0.05 * jnp.einsum(
        "nji,njk->nik", gradient, gradient, precision=highest
    )
    turned = jnp.einsum("nji,njk->nik", left_rot, gradient, precision=highest)
    turned = jnp.einsum("nij,njk->nik", turned, right_rot, precision=highest)
    moment_next = 0.5 * moment_old + 0.5 * turned
    second_next = 0.5 * second_old + 0.5 * turned * turned
    correct = 1.0 - 0.5**STEP
    ratio = moment_next / correct / (jnp.sqrt(second_next / correct) + 1e-08)
    stepped = jnp.einsum("nij,njk->nik", left_rot, ratio, precision=highest)
    stepped = jnp.einsum("nij,nkj->nik", stepped, right_rot, precision=highest)
    return (moment_next, second_next, left_next, right_next, weights - rate_matrix * stepped)


def adam_update(gradient, values, moment_old, second_old):
    moment_next = 0.5 * moment_old + 0.5 * gradient
    second_next = 0.5 * second_old + 0.5 * gradient * gradient
    correct = 1.0 - 0.5**STEP
    ratio = moment_next / correct / (jnp.sqrt(second_next / correct) + 1e-08)
    return (moment_next, second_next, values - rate_vector * ratio)


def masked_scores(joint_row, segment_row, length_row):
    positions = joint_row.shape[0]
    query = joint_row[:, 0].reshape(positions, -1, HD)
    keyed = joint_row[:, 1].reshape(positions, -1, HD)
    valued = joint_row[:, 2].reshape(positions, -1, HD)
    scores = jnp.einsum("qhd,khd->hqk", query, keyed, preferred_element_type=jnp.float32) * 0.125
    visible = passage_mask(segment_row, length_row)
    return (jnp.where(visible[None], scores, -1e30), query, keyed, valued)


def attend_rows(item):
    joint_row, segment_row, length_row = item
    scores, query, keyed, valued = masked_scores(joint_row, segment_row, length_row)
    largest = jnp.max(scores, axis=-1, keepdims=True)
    raised = jnp.exp(scores - largest)
    totals = jnp.sum(raised, axis=-1, keepdims=True)
    probs = raised / totals
    logsum = (largest + jnp.log(totals))[..., 0]
    context = jnp.einsum(
        "hqk,khd->qhd", probs.astype(jnp.bfloat16), valued, preferred_element_type=jnp.float32
    )
    return (context.reshape(joint_row.shape[0], -1).astype(jnp.bfloat16), logsum)


def back_rows(item):
    joint_row, logsum, delta_context, segment_row, length_row = item
    positions = joint_row.shape[0]
    scores, query, keyed, valued = masked_scores(joint_row, segment_row, length_row)
    probs = jnp.exp(scores - logsum[..., None])
    delta_ctx = delta_context.reshape(positions, -1, HD)
    delta_value = jnp.einsum(
        "hqk,qhd->khd", probs.astype(jnp.bfloat16), delta_ctx, preferred_element_type=jnp.float32
    )
    delta_prob = jnp.einsum("qhd,khd->hqk", delta_ctx, valued, preferred_element_type=jnp.float32)
    weighted = jnp.sum(probs * delta_prob, axis=-1, keepdims=True)
    delta_score = (probs * (delta_prob - weighted)).astype(jnp.bfloat16)
    delta_query = (
        jnp.einsum("hqk,khd->qhd", delta_score, keyed, preferred_element_type=jnp.float32) * 0.125
    )
    delta_key = (
        jnp.einsum("hqk,qhd->khd", delta_score, query, preferred_element_type=jnp.float32) * 0.125
    )
    stacked = jnp.stack(
        [
            delta_query.reshape(positions, -1),
            delta_key.reshape(positions, -1),
            delta_value.reshape(positions, -1),
        ],
        axis=1,
    )
    return stacked.astype(jnp.bfloat16)


def pick_blocks(source, slot_index, owner_slot, fanout, part_index):
    matches = owner_slot[None, :] == slot_index[:, None]
    present = jnp.any(matches, axis=1).astype(jnp.float32)
    chosen = jnp.sum(
        matches.astype(jnp.int32) * jnp.arange(owner_slot.shape[0], dtype=jnp.int32)[None, :],
        axis=1,
    )
    picked = jnp.take(source, chosen * fanout + part_index, axis=0)
    return picked * present[:, None, None]


def per_device(
    tokens,
    output_grad,
    segment_ids,
    lengths,
    owner_slot,
    slot_weights,
    first_moment,
    second_moment,
    left_stats,
    right_stats,
    left_basis,
    right_basis,
    vector_values,
    vector_first,
    vector_second,
):
    holding = slot_weights.shape[0]
    row_count = tokens.shape[0]
    token_count = tokens.shape[1]
    gathered, vector_half = (
        lax.all_gather(slot_weights.astype(jnp.bfloat16), "dp", axis=0, tiled=True),
        lax.all_gather(vector_values.astype(jnp.bfloat16), "dp", axis=0, tiled=True),
    )
    blocks = jnp.take(gathered, owner_slot, axis=0)
    w_query, w_key, w_value, w_output, w_upward, w_downward = split_blocks(blocks)
    w_joint = jnp.concatenate([w_query, w_key, w_value], axis=1)
    gains = vector_half.astype(jnp.float32).reshape(4, D)
    flat_tokens = tokens.reshape(-1, D)
    projected = jnp.dot(flat_tokens, w_joint, preferred_element_type=jnp.float32).astype(
        jnp.bfloat16
    )
    projected = projected.reshape(row_count, token_count, 3, D)
    heads = lax.all_to_all(projected, "sp", split_axis=3, concat_axis=1, tiled=True)
    context, logsum = lax.map(attend_rows, (heads, segment_ids, lengths))
    context_tok = lax.all_to_all(context, "sp", split_axis=1, concat_axis=2, tiled=True).reshape(
        -1, D
    )
    attended = jnp.dot(context_tok, w_output, preferred_element_type=jnp.float32)
    summed_one = flat_tokens.astype(jnp.float32) + attended
    hidden, norm_one_pull = jax.vjp(layer_norm, summed_one, gains[0], gains[1])
    hidden_half = hidden.astype(jnp.bfloat16)
    upward = jnp.dot(hidden_half, w_upward, preferred_element_type=jnp.float32)
    activated, gelu_pull = jax.vjp(exact_gelu, upward)
    active_half = activated.astype(jnp.bfloat16)
    downward = jnp.dot(active_half, w_downward, preferred_element_type=jnp.float32)
    result, norm_two_pull = jax.vjp(layer_norm, hidden + downward, gains[2], gains[3])
    block_out = result.astype(jnp.bfloat16).reshape(row_count, token_count, D)
    cotangent = output_grad.reshape(-1, D).astype(jnp.float32)
    delta_two, delta_gain_two, delta_shift_two = norm_two_pull(cotangent)
    delta_down = delta_two.astype(jnp.bfloat16)
    grad_down = contract_rows(active_half, delta_down)
    delta_active = contract_cols(delta_down, w_downward)
    (delta_upward,) = gelu_pull(delta_active)
    delta_up = delta_upward.astype(jnp.bfloat16)
    grad_up = contract_rows(hidden_half, delta_up)
    delta_hidden = delta_two + contract_cols(delta_up, w_upward)
    delta_one, delta_gain_one, delta_shift_one = norm_one_pull(delta_hidden)
    delta_attn = delta_one.astype(jnp.bfloat16)
    grad_output = contract_rows(context_tok, delta_attn)
    delta_context = (
        contract_cols(delta_attn, w_output).astype(jnp.bfloat16).reshape(row_count, token_count, D)
    )
    delta_heads = lax.all_to_all(delta_context, "sp", split_axis=2, concat_axis=1, tiled=True)
    delta_projected = lax.map(back_rows, (heads, logsum, delta_heads, segment_ids, lengths))
    delta_joint = lax.all_to_all(
        delta_projected, "sp", split_axis=1, concat_axis=3, tiled=True
    ).reshape(-1, 3 * D)
    grad_joint = contract_rows(flat_tokens, delta_joint)
    input_grad = (delta_one + contract_cols(delta_joint, w_joint)).reshape(
        row_count, token_count, D
    )
    grad_blocks = jnp.concatenate(
        [
            into_blocks(grad_joint[:, :D]),
            into_blocks(grad_joint[:, D : 2 * D]),
            into_blocks(grad_joint[:, 2 * D :]),
            into_blocks(grad_output),
            into_blocks(grad_up),
            into_blocks(grad_down),
        ],
        axis=0,
    )
    vector_grad = jnp.concatenate(
        [delta_gain_one, delta_shift_one, delta_gain_two, delta_shift_two]
    )
    vector_total = lax.psum(vector_grad, ("dp", "sp"))
    piece_len = vector_values.shape[0]
    vector_piece = lax.dynamic_slice_in_dim(
        vector_total, lax.axis_index("dp") * piece_len, piece_len
    )
    slot_index = jnp.arange(holding * lax.axis_size("dp"), dtype=jnp.int32)
    owned = lax.psum_scatter(
        pick_blocks(grad_blocks, slot_index, owner_slot, 1, 0),
        "dp",
        scatter_dimension=0,
        tiled=True,
    )
    owned = lax.psum(owned.astype(jnp.bfloat16), "sp").astype(jnp.float32)
    moment_one, moment_two, left_new, right_new, weights_new = soap_update(
        owned,
        slot_weights,
        first_moment,
        second_moment,
        left_stats,
        right_stats,
        left_basis,
        right_basis,
    )
    vector_one, vector_two, vector_new = adam_update(
        vector_piece, vector_values, vector_first, vector_second
    )
    return (
        block_out,
        input_grad,
        moment_one,
        moment_two,
        left_new,
        right_new,
        weights_new,
        weights_new.astype(jnp.bfloat16),
        vector_one,
        vector_two,
        vector_new,
    )


PITCH = BLK + 16
MESH = pl.DeviceIdType.MESH
NZ = 4


def in_hbm(value):
    return pltpu.with_memory_space_constraint(value, pltpu.HBM)


def place():
    dp = lax.axis_index("dp")
    sp = lax.axis_index("sp")
    return dp // 2, dp % 2, sp // 2, sp % 2


def greet(z, y, x, c):
    barrier = pltpu.get_barrier_semaphore()
    dp = z * 2 + y
    sp = x * 2 + c

    def signal(target):
        pl.semaphore_signal(barrier, 1, device_id=target, device_id_type=MESH)

    for step in range(1, 4):
        signal((dp, (sp + step) % 4))
    signal((z * 2 + 1 - y, sp))

    @pl.when(z < NZ - 1)
    def _():
        signal((dp + 2, sp))

    @pl.when(z > 0)
    def _():
        signal((dp - 2, sp))

    pl.semaphore_wait(barrier, 4 + (z < NZ - 1).astype(jnp.int32) + (z > 0).astype(jnp.int32))


PIECES = {
    "A0": (BLK + 16, False, True),
    "A1": (BLK // 2, False, False),
    "O0": (BLK // 2, True, True),
    "O1": (BLK // 4, True, True),
}
STEPS = (
    ("own", "O1"), ("rows", 1), ("own", "O0"), ("own", "A1"), ("z", "O1", 1, 1, 0), ("z", "O1", 1, -1, 0),
    ("y", "O1", 0, 0), ("z", "O0", 1, 1, 0), ("own", "A0"), ("z", "O0", 2, 1, 0), ("y", "O0", 0, 0),
    ("z", "O0", 1, -1, 0), ("z", "O1", 2, -1, 0), ("y", "O1", 1, -1), ("z", "O1", 3, -1, 0), ("z", "A1", 1, 1, 0),
    ("z", "O1", 2, 1, 0), ("y", "O1", 1, 1), ("z", "O0", 3, 1, 0), ("z", "A0", 1, -1, 0), ("y", "O1", 2, -1),
    ("y", "O0", 1, 1), ("z", "O1", 3, 1, 0), ("y", "O0", 2, 1), ("x", "O0", 3, 1, 0), ("x", "O1", 3, -1, 0),
    ("x", "O1", 1, 1, 0), ("z", "A1", 1, -1, 0), ("x", "O0", 1, -1, 0), ("z", "A0", 1, 1, 0),
    ("x", "O1", 1, -1, 1), ("y", "O1", 3, -1), ("y", "A1", 0, 0), ("z", "A0", 2, 1, 0), ("x", "O0", 2, 1, 0),
    ("y", "O1", 2, 1), ("rows", 0), ("z", "O0", 2, -1, 0), ("x", "O0", 2, 1, 1), ("z", "A0", 2, -1, 0),
    ("x", "O1", 0, 0, 1), ("z", "A1", 1, 1, 1), ("x", "O0", 1, 1, 1), ("z", "O0", 3, -1, 0), ("z", "A1", 1, -1, 1),
    ("y", "O0", 2, -1), ("y", "O0", 3, 1), ("y", "A0", 1, -1), ("x", "O1", 2, 1, 1), ("x", "O1", 3, 1, 0),
    ("x", "O0", 0, 0, 1), ("y", "O0", 3, -1), ("z", "A0", 3, 1, 0), ("y", "O1", 3, 1), ("z", "A0", 3, -1, 0),
    ("x", "O0", 1, 1, 0), ("x", "O1", 3, -1, 1), ("y", "O0", 1, -1), ("z", "A1", 2, -1, 0), ("y", "A0", 0, 0),
    ("x", "O1", 2, -1, 1), ("y", "A0", 2, -1), ("z", "A1", 2, -1, 1), ("x", "O0", 2, -1, 0), ("z", "A1", 3, -1, 0),
    ("x", "O0", 3, -1, 0), ("x", "O0", 3, -1, 1), ("z", "A1", 2, 1, 1), ("y", "A0", 2, 1), ("z", "A1", 2, 1, 0),
    ("x", "O0", 3, 1, 1), ("x", "O1", 2, -1, 0), ("z", "A1", 3, 1, 1), ("x", "O1", 2, 1, 0), ("x", "O0", 2, -1, 1),
    ("y", "A0", 3, -1), ("y", "A0", 1, 1), ("y", "A0", 3, 1), ("x", "O1", 3, 1, 1), ("x", "O1", 1, -1, 0),
    ("x", "O1", 1, 1, 1), ("x", "O0", 1, -1, 1), ("z", "A1", 3, -1, 1), ("z", "A1", 3, 1, 0),
)


def piece_view(ref, name, x_of, c_of, base):
    height = PIECES[name][0]
    if name == "A0":
        return ref.at[base + c_of, pl.ds(0, height)]
    if name == "A1":
        slot, row = base + 2, height * c_of
    elif name == "O0":
        slot, row = base + 4 + x_of, height * c_of
    else:
        slot, row = base + 3, 2 * height * x_of + height * c_of
    return ref.at[slot, pl.ds(pl.multiple_of(row, height), height)]


def gather_kernel(weights, vector, tokens, grads, out, token_row, grad_row, wide, narrow, *sems):
    z, y, x, c = place()
    dp = z * 2 + y
    sp = x * 2 + c
    sems = list(sems)
    load_sem, keep_sem, row_send, row_recv, row_keep = [sems.pop(0) for _ in range(5)]
    ways = ("up", "down", "y", "mate", "x", "pass")
    send_sem = {(way, name): sems.pop(0) for way in ways for name in PIECES if PIECES[name][1] or way not in ways[4:]}
    recv_sem = {(way, name): sems.pop(0) for way in ways[2:] for name in PIECES if PIECES[name][1] or way not in ways[4:]}
    targets = {
        "up": (dp + 2, sp), "down": (dp - 2, sp), "y": (z * 2 + 1 - y, sp),
        "x": (dp, (1 - x) * 2 + c), "mate": (dp, x * 2 + 1 - c), "pass": (dp, x * 2 + 1 - c),
    }
    def load_of(i):
        return pltpu.make_async_copy(weights.at[i], wide.at[i], load_sem.at[i])

    for i in (c, 2, 3, 4 + x, 1 - c, 5 - x):
        load_of(i).start()
    keeps = [
        pltpu.make_async_copy(tokens.at[sp], token_row.at[sp], row_keep.at[0]),
        pltpu.make_async_copy(grads.at[sp], grad_row.at[sp], row_keep.at[1]),
    ]
    for keep in keeps:
        keep.start()
    gains = jnp.broadcast_to(vector[...], (16, BLK)).astype(jnp.bfloat16)
    greet(z, y, x, c)

    def row_copy(which, source, landing, step, arrival):
        peer = (sp + step) % 4
        at = peer if arrival else sp
        return pltpu.make_async_remote_copy(
            src_ref=source.at[peer], dst_ref=landing.at[at],
            send_sem=row_send.at[which, step - 1], recv_sem=row_recv.at[which, at],
            device_id=(dp, peer), device_id_type=MESH,
        )

    def round_block(i):
        load_of(i).wait()
        narrow[i, :BLK, :] = wide[i].astype(jnp.bfloat16)
        narrow[i, BLK:, :] = gains

    for i in (c, 2, 3, 4 + x):
        round_block(i)
    own = [pltpu.make_async_copy(narrow.at[i], out.at[dp * 6 + i], keep_sem.at[i]) for i in range(6)]
    started = []

    def item_of(way, name, holder, x_of, c_of, fresh=False):
        landing = piece_view(out, name, x_of, c_of, holder * 6)
        arrives = way if way in ("mate", "x", "pass") else "y"
        return pltpu.make_async_remote_copy(
            src_ref=piece_view(narrow, name, x_of, c_of, 0) if fresh else landing, dst_ref=landing,
            send_sem=send_sem[way, name].at[holder], recv_sem=recv_sem[arrives, name].at[holder],
            device_id=targets[way], device_id_type=MESH,
        )

    def send(way, name, holder, valid, x_of=x, fresh=False):
        if way in ("up", "down"):
            room = z < NZ - 1 if way == "up" else z > 0
            valid = room if valid is None else valid & room
        item = item_of(way, name, holder, x_of, c, fresh)
        if valid is None:
            item.start()
        else:
            pl.when(valid)(item.start)
        started.append((item, valid))

    def arrive(way, name, holder, valid, x_of, c_of):
        item = item_of(way, name, holder, x_of, c_of)
        if valid is None:
            item.wait_recv()
        else:
            pl.when(valid)(item.wait_recv)

    def origin_of(sign, far):
        origin = z + sign * far
        if far == 0:
            return origin, None
        return origin, ((origin >= 0) if sign < 0 else (origin <= NZ - 1))

    for step in STEPS:
        kind, name = step[0], step[1]
        if kind == "own":
            for way in ("up", "down", "y"):
                send(way, name, dp, None, fresh=True)
        elif kind == "rows":
            source, landing = ((tokens, token_row), (grads, grad_row))[name]
            for hop in (2, 3, 1):
                row_copy(name, source, landing, hop, False).start()
        else:
            origin, inside = origin_of(step[3], step[2])
            if kind == "x":
                holder = origin * 2 + (y if step[4] == 0 else 1 - y)
                arrive("x", name, holder, inside, 1 - x, c)
                send("pass", name, holder, inside, 1 - x)
                continue
            holder = origin * 2 + (y if kind == "z" and step[4] == 0 else 1 - y)
            arrive("y", name, holder, inside, x, c)
            if kind == "z":
                if step[2] < NZ - 1:
                    send("up" if step[3] < 0 else "down", name, holder, inside)
                if PIECES[name][2] and step[4] == 0:
                    send("y", name, holder, inside)
            elif not PIECES[name][2]:
                send("up", name, holder, inside)
                send("down", name, holder, inside)
            if PIECES[name][1]:
                send("x", name, holder, inside)
            send("mate", name, holder, inside)
        if kind == "own" and name == "A0":
            for i in (1 - c, 5 - x):
                round_block(i)
            for item in own:
                item.start()

    for far in range(NZ):
        for sign in (0,) if far == 0 else (-1, 1):
            origin, inside = origin_of(sign, far)
            for column in (1,) if far == 0 else (0, 1):
                holder = origin * 2 + (y if column == 0 else 1 - y)
                for name in PIECES:
                    arrive("mate", name, holder, inside, x, 1 - c)
                    if PIECES[name][1]:
                        arrive("pass", name, holder, inside, 1 - x, 1 - c)
    for hop in (2, 3, 1):
        for which, source, landing in ((0, tokens, token_row), (1, grads, grad_row)):
            row_copy(which, source, landing, hop, True).wait_recv()
            row_copy(which, source, landing, hop, False).wait_send()
    for item, valid in started:
        if valid is None:
            item.wait_send()
        else:
            pl.when(valid)(item.wait_send)
    for item in own + keeps:
        item.wait()


def gather_all(weights, vector, tokens, grads):
    anywhere = pl.BlockSpec(memory_space=pl.ANY)
    dma = pltpu.SemaphoreType.DMA
    carried = sum(1 for name in PIECES if PIECES[name][1])
    flows = (4 * len(PIECES) + 2 * carried) + (2 * len(PIECES) + 2 * carried)
    return pl.pallas_call(
        gather_kernel,
        name="gather_all",
        out_shape=[
            pltpu.HBM((48, PITCH, BLK), jnp.bfloat16),
            pltpu.HBM(tokens.shape, jnp.bfloat16),
            pltpu.HBM(grads.shape, jnp.bfloat16),
        ],
        in_specs=[anywhere, pl.BlockSpec(memory_space=pltpu.VMEM), anywhere, anywhere],
        out_specs=[anywhere, anywhere, anywhere],
        scratch_shapes=[
            pltpu.VMEM((6, BLK, BLK), jnp.float32),
            pltpu.VMEM((6, PITCH, BLK), jnp.bfloat16),
            dma((6,)), dma((6,)), dma((2, 3)), dma((2, 4)), dma((2,)),
        ]
        + [dma((8,))] * flows,
        compiler_params=pltpu.CompilerParams(
            collective_id=0, has_side_effects=True, vmem_limit_bytes=24 << 20
        ),
    )(in_hbm(weights), vector.reshape(1, BLK), in_hbm(tokens), in_hbm(grads))


ROW = 512
PAIR = 128
SPAN = 384
EPS = 1e-06


def gelu_of(u):
    bell = jnp.exp(-0.5 * u * u)
    t = 1.0 / (1.0 + (0.3275911 / math.sqrt(2.0)) * jnp.abs(u))
    tail = 0.5 * 1.061405429
    for term in (-1.453152027, 1.421413741, -0.284496736, 0.254829592):
        tail = tail * t + 0.5 * term
    tail = tail * t * bell
    below = jnp.where(u >= 0.0, 1.0 - tail, tail)
    return (u * below).astype(jnp.bfloat16), below + u * (bell * (1.0 / math.sqrt(2.0 * math.pi)))


def dot_nn(a, b):
    return lax.dot_general(a, b, (((1,), (0,)), ((), ())), preferred_element_type=jnp.float32)


def dot_nt(a, b):
    return lax.dot_general(a, b, (((1,), (1,)), ((), ())), preferred_element_type=jnp.float32)


def dot_tn(a, b):
    return lax.dot_general(a, b, (((0,), (0,)), ((), ())), preferred_element_type=jnp.float32)


def layer_kernel(
    owner, weights, tokens, dy_ref, segments, grads, block_out, input_half,
    wqkv, wo, w1, w2, gains, qkv, probs, shares, held, context, hidden, hidden16, norm1, act, slope, dz, dz16,
    dqkv, dup, stage, flipped, flipped_hidden, ups, vecs, spread, w_sem, g_sem, v_sem,
):
    half = jnp.bfloat16
    sp = lax.axis_index("sp")

    def weight_copies():
        copies = []
        for which, ref in enumerate((wqkv.at[0], wqkv.at[1], wqkv.at[2], wo)):
            for r in range(2):
                for q in range(2):
                    copies.append((which * 4 + r * 2 + q, ref, r, q))
        for r in range(2):
            for q in range(8):
                copies.append((16 + r * 8 + q, w1.at[q // 2], r, q % 2))
        for r in range(8):
            for q in range(2):
                copies.append((32 + r * 2 + q, w2.at[r // 2], r % 2, q))
        return [
            pltpu.make_async_copy(
                weights.at[owner[b], pl.ds(0, BLK)],
                ref.at[pl.ds(r * BLK, BLK), pl.ds(q * BLK, BLK)],
                w_sem.at[b],
            )
            for b, ref, r, q in copies
        ]

    copies = weight_copies()
    gain_copies = [
        pltpu.make_async_copy(
            weights.at[6 * d, pl.ds(BLK, 16)], gains.at[d // 2, :, pl.ds((d % 2) * BLK, BLK)], g_sem.at[d]
        )
        for d in range(8)
    ]
    for item in copies[:16] + gain_copies + copies[16:]:
        item.start()

    seg_row = segments[pl.ds(sp, 1), :].astype(jnp.float32)
    spread[...] = jnp.transpose(jnp.broadcast_to(seg_row, (PAIR, ROW)))

    for item in copies[:12]:
        item.wait()
    x = tokens[...]
    flipped[...] = jnp.transpose(x)
    for part in range(3):
        block = dot_nn(x, wqkv[part])
        if part == 0:
            block = block * 0.125
        block = block.astype(half)
        for p in range(6):
            qkv[part * 6 + p] = block[:, p * PAIR : (p + 1) * PAIR]

    lane = lax.broadcasted_iota(jnp.int32, (1, PAIR), 1)
    lows = (lane < 64, lane >= 64)

    def visible(part):
        keys = segments[pl.ds(sp, 1), pl.ds(part * PAIR, SPAN)].astype(jnp.float32)
        own = spread[pl.ds(part * 256, 256), pl.ds(0, 1)]
        return own == keys

    def attend(p, carry):
        q2, k2, v2 = qkv[p], qkv[6 + p], qkv[12 + p]
        for part in range(2):
            mask = visible(part)
            qs = q2[part * 256 : part * 256 + 256]
            ks = k2[part * PAIR : part * PAIR + SPAN]
            vs = v2[part * PAIR : part * PAIR + SPAN]
            outs = []
            for h in range(2):
                scores = dot_nt(jnp.where(lows[h], qs, jnp.zeros_like(qs)), ks)
                scores = jnp.where(mask, scores, -1e30)
                raised = jnp.exp(scores - jnp.max(scores, axis=1, keepdims=True)).astype(half)
                probs[p, 2 * part + h] = raised
                outs.append(dot_nn(raised, jnp.where(lows[h], vs, jnp.ones_like(vs))))
            inverse = 1.0 / pltpu.roll(jnp.where(lows[0], outs[1], outs[0]), 64, 1)
            shares[p, pl.ds(part * 256, 256)] = inverse
            context[p, pl.ds(part * 256, 256)] = (jnp.where(lows[0], outs[0], outs[1]) * inverse).astype(half)
        return carry

    lax.fori_loop(0, 6, attend, 0, unroll=3)

    for item in copies[12:16] + gain_copies:
        item.wait()
    joined = jnp.concatenate([context[p] for p in range(6)], axis=1)

    def gain(k):
        return gains[k, pl.ds(0, 1), :].astype(jnp.float32)

    def normalise(z):
        centre = jnp.mean(z, axis=1, keepdims=True)
        z = z - centre
        inverse = lax.rsqrt(jnp.mean(z * z, axis=1, keepdims=True) + EPS)
        return z * inverse, inverse

    dz[...] = dot_nn(joined, wo[...])

    def norm_one(t, carry):
        rows = pl.ds(pl.multiple_of(t * 128, 128), 128)
        hat, inverse = normalise(tokens[rows, :].astype(jnp.float32) + dz[rows, :])
        norm1[rows, :] = hat
        spread[rows, :] = jnp.where(lane == 1, inverse, spread[rows, :])
        value = hat * gain(0) + gain(1)
        hidden[rows, :] = value
        hidden16[rows, :] = value.astype(half)
        return carry

    lax.fori_loop(0, 4, norm_one, 0)
    for item in copies[16:]:
        item.wait()

    flipped_hidden[...] = jnp.transpose(hidden16[...])
    ups[0] = dot_nn(hidden16[...], w1[0])
    for j in range(5):
        if j < 3:
            ups[(j + 1) % 2] = dot_nn(hidden16[...], w1[j + 1])
        if j < 4:
            act[j], slope[j] = gelu_of(ups[j % 2])
        if j > 0:
            hidden[...] += dot_nn(act[j - 1], w2[j - 1])

    vecs[...] = jnp.zeros_like(vecs)

    def fold(value):
        return jnp.sum(value.reshape(-1, 8, D), axis=0)

    def norm_back(hat, inverse, delta, gain_row):
        e = delta * gain_row
        return (
            e - jnp.mean(e, axis=1, keepdims=True) - hat * jnp.mean(e * hat, axis=1, keepdims=True)
        ) * inverse

    def norm_two(t, carry):
        rows = pl.ds(pl.multiple_of(t * 128, 128), 128)
        hat, inverse = normalise(hidden[rows, :])
        block_out[rows, :] = (hat * gain(2) + gain(3)).astype(half)
        delta = dy_ref[rows, :].astype(jnp.float32)
        vecs[2] += fold(delta * hat)
        vecs[3] += fold(delta)
        back = norm_back(hat, inverse, delta, gain(2))
        dz[rows, :] = back
        dz16[rows, :] = back.astype(half)
        return carry

    lax.fori_loop(0, 4, norm_two, 0)

    def out_copy(slot, b, r, q):
        return pltpu.make_async_copy(
            stage.at[slot, pl.ds(r * BLK, BLK), pl.ds(q * BLK, BLK)],
            grads.at[owner[b], pl.ds(0, BLK)],
            v_sem.at[slot, r * 2 + q],
        )

    def flush(slot, blocks):
        for r in range(2):
            for q in range(2):
                out_copy(slot, blocks(r, q), r, q).start()

    def drain(slot):
        for r in range(2):
            for q in range(2):
                out_copy(slot, 0, r, q).wait()

    def backward(pair, carry):
        @pl.when(pair > 0)
        def _():
            for slot in range(4):
                drain(slot)

        ddown = dz16[...]
        for k in range(2):
            j = 2 * pair + k
            delta = (dot_nt(ddown, w2[j]) * slope[j]).astype(half)
            stage[2 * k] = dot_tn(act[j], ddown).astype(half)
            stage[2 * k + 1] = dot_nn(flipped_hidden[...], delta).astype(half)
            dz[...] += dot_nt(delta, w1[j])
        for k in range(2):
            j = 2 * pair + k
            flush(2 * k, lambda r, q: 32 + (2 * j + r) * 2 + q)
            flush(2 * k + 1, lambda r, q: 16 + r * 8 + 2 * j + q)
        return carry

    lax.fori_loop(0, 2, backward, 0)

    def norm_one_back(t, carry):
        rows = pl.ds(pl.multiple_of(t * 128, 128), 128)
        hat = norm1[rows, :]
        delta = dz[rows, :]
        vecs[0] += fold(delta * hat)
        vecs[1] += fold(delta)
        back = norm_back(hat, spread[rows, pl.ds(1, 1)], delta, gain(0))
        dz[rows, :] = back
        dz16[rows, :] = back.astype(half)
        return carry

    lax.fori_loop(0, 4, norm_one_back, 0)

    for slot in range(4):
        drain(slot)
    dattn = dz16[...]
    stage[0] = dot_tn(joined, dattn).astype(half)
    flush(0, lambda r, q: 12 + r * 2 + q)
    dcontext = dot_nt(dattn, wo[...]).astype(half)
    for p in range(6):
        held[p] = context[p]
        context[p] = dcontext[:, p * PAIR : (p + 1) * PAIR]

    def attend_back(p, carry):
        q2, k2, v2, d2 = qkv[p], qkv[6 + p], qkv[12 + p], context[p]
        dup[...] = jnp.zeros_like(dup)
        for part in range(2):
            window = pl.ds(part * PAIR, SPAN)
            qs = q2[part * 256 : part * 256 + 256]
            ds = d2[part * 256 : part * 256 + 256]
            ks = k2[part * PAIR : part * PAIR + SPAN]
            vs = v2[part * PAIR : part * PAIR + SPAN]
            dvs, dqs, dks = [], [], []
            share = shares[p, pl.ds(part * 256, 256)]
            scaled = (ds.astype(jnp.float32) * share).astype(half)
            weight = scaled.astype(jnp.float32) * held[p, pl.ds(part * 256, 256)].astype(jnp.float32)
            for h in range(2):
                raised = probs[p, 2 * part + h]
                dprob = dot_nt(jnp.where(lows[h], scaled, jnp.zeros_like(scaled)), vs)
                centre = jnp.sum(jnp.where(lows[h], weight, 0.0), axis=1, keepdims=True)
                dscore = (raised.astype(jnp.float32) * (dprob - centre)).astype(half)
                dvs.append(dot_tn(raised, scaled))
                dqs.append(dot_nn(dscore, ks))
                dks.append(dot_tn(dscore, qs))
            dqkv[p, pl.ds(part * 256, 256)] = (
                jnp.where(lows[0], dqs[0], dqs[1]) * 0.125
            ).astype(half)
            dup[0, window] += jnp.where(lows[0], dks[0], dks[1])
            dup[1, window] += jnp.where(lows[0], dvs[0], dvs[1])
        dqkv[6 + p] = dup[0].astype(half)
        dqkv[12 + p] = dup[1].astype(half)
        return carry

    lax.fori_loop(0, 6, attend_back, 0, unroll=3)

    for part in range(3):
        delta = jnp.concatenate([dqkv[part * 6 + p] for p in range(6)], axis=1)
        stage[1 + part] = dot_nn(flipped[...], delta).astype(half)
        flush(1 + part, lambda r, q: part * 4 + r * 2 + q)
        dz[...] += dot_nt(delta, wqkv[part])

    input_half[...] = dz[...].astype(half)
    for k in range(4):
        row = jnp.sum(vecs[k], axis=0, keepdims=True)
        vecs16 = jnp.broadcast_to(row, (16, D)).astype(half)
        gains[k] = vecs16
    for k in range(4):
        for q in range(2):
            for s in range(2):
                pltpu.make_async_copy(
                    gains.at[k, :, pl.ds(q * BLK, BLK)],
                    grads.at[6 * (2 * k + q) + s, pl.ds(BLK, 16)],
                    w_sem.at[(2 * k + q) * 2 + s],
                ).start()
    for k in range(4):
        for q in range(2):
            for s in range(2):
                pltpu.make_async_copy(
                    gains.at[k, :, pl.ds(q * BLK, BLK)],
                    grads.at[6 * (2 * k + q) + s, pl.ds(BLK, 16)],
                    w_sem.at[(2 * k + q) * 2 + s],
                ).wait()
    for slot in range(4):
        drain(slot)


def run_layer(owner_slot, gathered, token_row, grad_row, segment_ids):
    half, full = jnp.bfloat16, jnp.float32
    anywhere = pl.BlockSpec(memory_space=pltpu.HBM)
    vmem = pl.BlockSpec(memory_space=pltpu.VMEM)
    dma = pltpu.SemaphoreType.DMA
    return pl.pallas_call(
        layer_kernel,
        name="run_layer",
        out_shape=[
            jax.ShapeDtypeStruct((48, PITCH, BLK), half),
            jax.ShapeDtypeStruct((ROW, D), half),
            jax.ShapeDtypeStruct((ROW, D), half),
        ],
        in_specs=[pl.BlockSpec(memory_space=pltpu.SMEM), anywhere, vmem, vmem, vmem],
        out_specs=[anywhere, vmem, vmem],
        scratch_shapes=[
            pltpu.VMEM((3, D, D), half),
            pltpu.VMEM((D, D), half),
            pltpu.VMEM((4, D, D), half),
            pltpu.VMEM((4, D, D), half),
            pltpu.VMEM((4, 16, D), half),
            pltpu.VMEM((18, ROW, PAIR), half),
            pltpu.VMEM((6, 4, 256, SPAN), half),
            pltpu.VMEM((6, ROW, PAIR), full),
            pltpu.VMEM((6, ROW, PAIR), half),
            pltpu.VMEM((6, ROW, PAIR), half),
            pltpu.VMEM((ROW, D), full),
            pltpu.VMEM((ROW, D), half),
            pltpu.VMEM((ROW, D), full),
            pltpu.VMEM((4, ROW, D), half),
            pltpu.VMEM((4, ROW, D), full),
            pltpu.VMEM((ROW, D), full),
            pltpu.VMEM((ROW, D), half),
            pltpu.VMEM((18, ROW, PAIR), half),
            pltpu.VMEM((2, ROW, PAIR), full),
            pltpu.VMEM((4, D, D), half),
            pltpu.VMEM((D, ROW), half),
            pltpu.VMEM((D, ROW), half),
            pltpu.VMEM((2, ROW, D), full),
            pltpu.VMEM((4, 8, D), full),
            pltpu.VMEM((ROW, PAIR), full),
            dma((48,)),
            dma((8,)),
            dma((4, 4)),
        ],
        compiler_params=pltpu.CompilerParams(vmem_limit_bytes=58 << 20),
    )(owner_slot, gathered, token_row, grad_row, segment_ids)


BLANK = BLK + 16
HALF = BLK // 2
STREAMS = {
    "A0": (BLANK, 0, True, True),
    "A1": (HALF, 0, True, True),
    "A2": (HALF, HALF, True, False),
    "O": (HALF, 0, False, True),
    "XO": (HALF, 0, False, True),
}
TASKS = (
    ("Y", "A1", 3), ("Z", "A2", 0, 1), ("Y", "A0", 0), ("X", "O", 0, 1), ("Z", "A2", 0, 0), ("X", "O", 2, 1),
    ("X", "O", 1, 0), ("Y", "A0", 1), ("Z", "A2", 1, 1), ("Y", "A0", 2), ("Z", "A2", 2, 0), ("X", "O", 0, 0),
    ("X", "O", 3, 0), ("Y", "O", 0), ("C", "A0", 0), ("Z", "A2", 2, 1), ("X", "O", 1, 1), ("Y", "O", 2),
    ("Y", "A0", 3), ("X", "O", 3, 1), ("X", "O", 2, 0), ("C", "A0", 1), ("R", 1), ("Y", "O", 1), ("Y", "A1", 0),
    ("C", "A1", 3), ("Z", "A2", 3, 1), ("Y", "O", 3), ("C", "O", 0), ("R", 0), ("C", "A0", 2), ("Y", "A1", 1),
    ("C", "A0", 3), ("C", "O", 2), ("Y", "A1", 2), ("C", "O", 1), ("F", "A0"), ("F1", "A2"), ("C", "A1", 0),
    ("C", "O", 3), ("Z", "A2", 3, 0), ("F", "O"), ("Z", "A2", 1, 0), ("C", "A1", 1), ("C", "A1", 2), ("F", "A2"),
    ("L", "O"), ("F", "A1"), ("L", "A0"), ("L", "A2"), ("L", "A1"),
)


def reduce_kernel(grads, rows_a, rows_b, total, land_a, land_b, *scratch):
    z, y, x, c = place()
    dp = z * 2 + y
    sp = x * 2 + c
    names = list(STREAMS)
    moving = [name for name in names if name != "XO"]
    planes = [name for name in moving if STREAMS[name][2]]
    scratch = list(scratch)

    def take(keys):
        return {key: scratch.pop(0) for key in keys}

    mine, core, side, line, last = take(names), take(names), take(moving), take(moving), take(planes)
    cross, = take(["cross"]).values()
    load_sem, core_send, core_recv = take(names), take(names), take(names)
    y_send, y_recv, z_send, z_recv = take(moving), take(moving), take(moving), take(moving)
    x_send, x_recv, last_send, last_recv, give_send, give_recv, keep_sem, row_send, row_recv, row_keep = scratch
    high = z // 2
    order = (3 - 3 * high, 2 - high, 1 - z + 4 * high, z)
    twin = (dp, (1 - x) * 2 + c)
    mate = (dp, x * 2 + 1 - c)
    beside = (z * 2 + 1 - y, sp)
    inner = (z > 0) & (z < NZ - 1)

    def view(ref, name, dest, core_of):
        base = dest * 6
        if name == "A0":
            return ref.at[base + core_of, pl.ds(0, BLANK)]
        if name in ("A1", "A2"):
            return ref.at[base + 2 + core_of, pl.ds(STREAMS[name][1], HALF)]
        slot = base + (4 + x if name == "O" else 5 - x)
        return ref.at[slot, pl.ds(pl.multiple_of(core_of * HALF, HALF), HALF)]

    def remote(src, dst, send, recv, target):
        return pltpu.make_async_remote_copy(
            src_ref=src, dst_ref=dst, send_sem=send, recv_sem=recv,
            device_id=target, device_id_type=MESH,
        )

    def load(name, dest):
        return pltpu.make_async_copy(view(grads, name, dest, c), mine[name].at[dest], load_sem[name].at[dest])

    def to_mate(name, dest):
        return remote(
            view(grads, name, dest, 1 - c), core[name].at[dest],
            core_send[name].at[dest], core_recv[name].at[dest], mate,
        )

    def to_twin(dest):
        return remote(mine["XO"].at[dest], cross.at[dest], x_send.at[dest], x_recv.at[dest], twin)

    def to_side(name, goal):
        at = goal if STREAMS[name][3] else 0
        return remote(
            mine[name].at[goal * 2 + 1 - y], side[name].at[at],
            y_send[name].at[at], y_recv[name].at[at], beside,
        )

    def row_copy(which, source, landing, step, arrival):
        peer = (sp + step) % 4
        at = peer if arrival else sp
        return remote(
            source.at[peer], landing.at[at],
            row_send.at[which, step - 1], row_recv.at[which, at], (dp, peer),
        )

    def column_of(flag):
        return y if flag == 0 else 1 - y

    def dest_of(task):
        if task[0] in ("X", "Z"):
            return order[task[2]] * 2 + column_of(task[3])
        return order[task[2]] * 2 + (1 - y if task[0] == "Y" else y)

    sequence = [
        ("XO" if task[0] == "X" else task[1], dest_of(task)) for task in TASKS if task[0] in ("X", "Y", "C", "Z")
    ]
    for name, dest in sequence:
        load(name, dest).start()
    keeps = [
        pltpu.make_async_copy(rows_a.at[sp], land_a.at[sp], row_keep.at[0]),
        pltpu.make_async_copy(rows_b.at[sp], land_b.at[sp], row_keep.at[1]),
    ]
    for keep in keeps:
        keep.start()
    greet(z, y, x, c)
    for name, dest in sequence:
        to_mate(name, dest).start()

    def merge(name, dest):
        load(name, dest).wait()
        to_mate(name, dest).wait_recv()
        value = mine[name][dest] + core[name][dest]
        if name == "O":
            to_twin(dest).wait_recv()
            value = value + cross[dest]
        mine[name][dest] = value

    def hop(name, goal, column, way, target):
        lane = goal if STREAMS[name][3] else goal * 2 + column
        return remote(
            mine[name].at[goal * 2 + column], line[name].at[way, lane],
            z_send[name].at[lane], z_recv[name].at[way, lane], target,
        )

    def along(name, goal, column):
        dest = goal * 2 + column
        upward = (goal > z).astype(jnp.int32)
        step = 2 * upward - 1
        way = 1 - upward
        item = hop(name, goal, column, way, (dp + 2 * step, sp))
        lane = goal if STREAMS[name][3] else dest

        @pl.when(inner)
        def _():
            item.wait_recv()
            mine[name][dest] = mine[name][dest] + line[name][way, lane]

        item.start()

    def settle(name, column):
        dest = z * 2 + column
        lane = z if STREAMS[name][3] else dest
        for way, valid, step in ((0, z > 0, 1), (1, z < NZ - 1, -1)):
            @pl.when(valid)
            def _():
                hop(name, z, column, way, (dp - 2 * step, sp)).wait_recv()
                mine[name][dest] = mine[name][dest] + line[name][way, lane]

    def swap_last(name):
        at = planes.index(name)
        return remote(mine[name].at[dp], last[name], last_send.at[at], last_recv.at[at], twin)

    def place_of(name, core_of):
        return view(total, name, 0, core_of)

    gift_at = {name: at for at, name in enumerate(planes + ["O", "twin", "XO"])}

    def give(name, key, target, source, core_of):
        at = gift_at[key]
        return remote(source, place_of(name, core_of), give_send.at[at], give_recv.at[at], target)

    gifts, kept = [], []

    def hand_on(name, key, target, source):
        item = give(name, key, target, source, c)
        item.start()
        gifts.append(item)

    def keep_here(name, source):
        item = pltpu.make_async_copy(source, place_of(name, c), keep_sem.at[gift_at[name]])
        item.start()
        kept.append(item)

    for task in TASKS:
        kind, name = task[0], task[1]
        if kind == "R":
            source, landing = ((rows_a, land_a), (rows_b, land_b))[name]
            for step in (2, 3, 1):
                row_copy(name, source, landing, step, False).start()
        elif kind == "X":
            merge("XO", dest_of(task))
            to_twin(dest_of(task)).start()
        elif kind == "Y":
            merge(name, dest_of(task))
            to_side(name, order[task[2]]).start()
        elif kind == "C":
            dest = dest_of(task)
            merge(name, dest)
            to_side(name, order[task[2]]).wait_recv()
            mine[name][dest] = mine[name][dest] + side[name][order[task[2]]]
            if task[2] < 3:
                along(name, order[task[2]], y)
        elif kind == "Z":
            merge(name, dest_of(task))
            if task[2] < 3:
                along(name, order[task[2]], column_of(task[3]))
        elif kind == "F1":
            settle(name, 1 - y)
            to_side(name, z).start()
        elif kind == "F":
            settle(name, y)
            if not STREAMS[name][3]:
                to_side(name, z).wait_recv()
                mine[name][dp] = mine[name][dp] + side[name][0]
            if name in planes:
                swap_last(name).start()
            else:
                hand_on(name, "twin", twin, mine[name].at[dp])
                hand_on(name, "O", mate, mine[name].at[dp])
                keep_here(name, mine[name].at[dp])
        elif kind == "L":
            if name in planes:
                swap_last(name).wait_recv()
                core[name][dp] = mine[name][dp] + last[name][...]
                hand_on(name, name, mate, core[name].at[dp])
                keep_here(name, core[name].at[dp])
            else:
                give("XO", "twin", twin, place_of("XO", c), c).wait_recv()
                hand_on("XO", "XO", mate, place_of("XO", c))

    for name in planes + ["O", "XO"]:
        give(name, name, mate, place_of(name, 1 - c), 1 - c).wait_recv()
    for step in (2, 3, 1):
        for which, source, landing in ((0, rows_a, land_a), (1, rows_b, land_b)):
            row_copy(which, source, landing, step, True).wait_recv()
            row_copy(which, source, landing, step, False).wait_send()
    for name, dest in sequence:
        to_mate(name, dest).wait_send()
    for i in range(4):
        for column in (0, 1):
            to_twin(order[i] * 2 + column).wait_send()
        for name in moving:
            if STREAMS[name][3]:
                to_side(name, order[i]).wait_send()
                if i < 3:
                    hop(name, order[i], y, 0, twin).wait_send()
            elif i < 3:
                for column in (0, 1):
                    hop(name, order[i], column, 0, twin).wait_send()
            else:
                to_side(name, z).wait_send()
    for name in planes:
        swap_last(name).wait_send()
    for item in gifts:
        item.wait_send()
    for item in kept + keeps:
        item.wait()


def reduce_all(grads, rows_a, rows_b):
    anywhere = pl.BlockSpec(memory_space=pl.ANY)
    half = jnp.bfloat16
    dma = pltpu.SemaphoreType.DMA
    moving = [name for name in STREAMS if name != "XO"]
    planes = [name for name in moving if STREAMS[name][2]]

    def buffers(shapes):
        return [pltpu.VMEM((*lead, STREAMS[name][0], BLK), half) for name, lead in shapes]

    first = {name: STREAMS[name][3] for name in moving}
    return pl.pallas_call(
        reduce_kernel,
        name="reduce_all",
        out_shape=[
            jax.ShapeDtypeStruct((6, PITCH, BLK), half),
            pltpu.HBM(rows_a.shape, half),
            pltpu.HBM(rows_b.shape, half),
        ],
        in_specs=[anywhere] * 3,
        out_specs=[anywhere] * 3,
        scratch_shapes=buffers([(name, (8,)) for name in STREAMS] * 2)
        + buffers([(name, (4 if first[name] else 1,)) for name in moving])
        + buffers([(name, (2, 4 if first[name] else 8)) for name in moving])
        + buffers([(name, ()) for name in planes])
        + buffers([("O", (8,))])
        + [dma((8,))] * (3 * len(STREAMS))
        + [dma((4 if first[name] else 1,)) for name in moving] * 2
        + [dma((4 if first[name] else 8,)) for name in moving]
        + [dma((2, 4 if first[name] else 8)) for name in moving]
        + [
            dma((8,)), dma((8,)), dma((len(planes),)), dma((len(planes),)), dma((len(planes) + 3,)),
            dma((len(planes) + 3,)), dma((len(planes) + 1,)), dma((2, 3)), dma((2, 4)), dma((2,)),
        ],
        compiler_params=pltpu.CompilerParams(
            collective_id=1, has_side_effects=True, vmem_limit_bytes=28 << 20
        ),
    )(in_hbm(grads), in_hbm(rows_a), in_hbm(rows_b))


CORRECT = 1.0 - 0.5**STEP
GROUP = 2


def update_kernel(
    total, weights, first, second, left_old, right_old, left_rot, right_rot, vec, vec_first, vec_second, land_a,
    land_b, moment_one, moment_two, left_new, right_new, weights_new, weights_half, vector_one, vector_two, vector_new,
    rows_a, rows_b, held, narrow, wide, stage, stage_half, left, right, out_sem, in_sem, sems,
):
    half = jnp.bfloat16
    take_a = pltpu.make_async_copy(land_a, held, sems.at[0])
    give_a = pltpu.make_async_copy(held, rows_a, sems.at[3])
    take_b = pltpu.make_async_copy(land_b, narrow, sems.at[1])
    give_b = pltpu.make_async_copy(wide, rows_b, sems.at[2])
    count = weights.shape[0]

    def state_of(i):
        return [
            pltpu.make_async_copy(old.at[i], now.at[i], in_sem.at[i, k])
            for k, (old, now) in enumerate(((left_old, left), (right_old, right)))
        ]

    for i in range(count):
        for item in state_of(i):
            item.start()
    take_b.start()
    take_a.start()
    slope = total[0, pl.ds(BLK, 1), :].astype(jnp.float32).reshape(BLK)
    vec_one = 0.5 * vec_first[...] + 0.5 * slope
    vec_two = 0.5 * vec_second[...] + 0.5 * slope * slope
    vector_one[...] = vec_one
    vector_two[...] = vec_two
    vector_new[...] = vec[...] - rate_vector * (
        (vec_one / CORRECT) / (jnp.sqrt(vec_two / CORRECT) + 1e-08)
    )
    targets = (left_new, right_new, moment_one, moment_two, weights_new)

    def outputs(i):
        copies = [
            pltpu.make_async_copy(stage.at[k, i], target.at[i], out_sem.at[i, k])
            for k, target in enumerate(targets)
        ]
        return copies + [pltpu.make_async_copy(stage_half.at[i], weights_half.at[i], out_sem.at[i, 5])]

    def blocks(pair, carry):
        for i in [pair * GROUP + k for k in range(GROUP)]:
            for item in state_of(i):
                item.wait()
        for i in [pair * GROUP + k for k in range(GROUP)]:
            grad = total[i, :BLK, :]
            rot_l = left_rot[i].astype(half)
            rot_r = right_rot[i].astype(half)
            turned = dot_nn(dot_tn(rot_l, grad).astype(half), rot_r)
            stage[0, i] = 0.95 * left[i] + 0.05 * dot_nt(grad, grad)
            one = 0.5 * first[i] + 0.5 * turned
            two = 0.5 * second[i] + 0.5 * turned * turned
            stage[2, i] = one
            stage[3, i] = two
            spread = two * (1.0 / CORRECT)
            ratio = (one * (1.0 / CORRECT)) / (spread * lax.rsqrt(spread) + 1e-08)
            stage[1, i] = 0.95 * right[i] + 0.05 * dot_tn(grad, grad)
            stepped = dot_nt(dot_nn(rot_l, ratio.astype(half)).astype(half), rot_r)
            fresh = weights[i] - rate_matrix * stepped
            stage[4, i] = fresh
            stage_half[i] = fresh.astype(half)
        for i in [pair * GROUP + k for k in range(GROUP)]:
            for item in outputs(i):
                item.start()

        @pl.when(pair == 0)
        def _():
            take_a.wait()
            give_a.start()
            take_b.wait()
            for r in range(narrow.shape[0]):
                wide[r] = narrow[r].astype(jnp.float32)
            give_b.start()

        return carry

    lax.fori_loop(0, weights.shape[0] // GROUP, blocks, 0)
    for i in range(weights.shape[0]):
        for item in outputs(i):
            item.wait()
    give_a.wait()
    give_b.wait()


def update_all(
    total, weights, first, second, left, right, left_rot, right_rot, vec, vec_first, vec_second, land_a, land_b
):
    full = jnp.float32
    vmem = pl.BlockSpec(memory_space=pltpu.VMEM)
    anywhere = pl.BlockSpec(memory_space=pl.ANY)
    vector = jax.ShapeDtypeStruct((BLK,), full)
    matrix = pltpu.HBM(weights.shape, full)
    return pl.pallas_call(
        update_kernel,
        name="update_all",
        out_shape=[matrix] * 5 + [pltpu.HBM(weights.shape, jnp.bfloat16)] + [vector] * 3
        + [pltpu.HBM(land_a.shape, jnp.bfloat16), pltpu.HBM(land_b.shape, full)],
        in_specs=[vmem] * 4 + [anywhere] * 2 + [vmem] * 5 + [anywhere] * 2,
        out_specs=[anywhere] * 6 + [vmem] * 3 + [anywhere] * 2,
        scratch_shapes=[
            pltpu.VMEM(land_a.shape, jnp.bfloat16),
            pltpu.VMEM(land_b.shape, jnp.bfloat16),
            pltpu.VMEM(land_b.shape, full),
            pltpu.VMEM((5, *weights.shape), full),
            pltpu.VMEM(weights.shape, jnp.bfloat16),
            pltpu.VMEM(weights.shape, full),
            pltpu.VMEM(weights.shape, full),
            pltpu.SemaphoreType.DMA((weights.shape[0], 6)),
            pltpu.SemaphoreType.DMA((weights.shape[0], 2)),
            pltpu.SemaphoreType.DMA((4,)),
        ],
        compiler_params=pltpu.CompilerParams(vmem_limit_bytes=38 << 20),
    )(
        total, weights, first, second, in_hbm(left), in_hbm(right), left_rot, right_rot,
        vec, vec_first, vec_second, in_hbm(land_a), in_hbm(land_b),
    )


def fast_device(
    tokens, output_grad, segment_ids, lengths, owner_slot, slot_weights, first_moment, second_moment,
    left_stats, right_stats, left_basis, right_basis, vector_values, vector_first, vector_second,
):
    gathered, token_row, grad_row = gather_all(slot_weights, vector_values, tokens, output_grad)
    placed, block_row, input_row = run_layer(
        owner_slot, gathered, token_row.reshape(-1, D), grad_row.reshape(-1, D), segment_ids
    )
    total, block_land, input_land = reduce_all(
        placed, block_row.reshape(tokens.shape), input_row.reshape(tokens.shape)
    )
    updated = update_all(
        total, slot_weights, first_moment, second_moment, left_stats, right_stats, left_basis, right_basis,
        vector_values, vector_first, vector_second, block_land, input_land,
    )
    vectors = [value.reshape(-1) for value in updated[6:9]]
    return (updated[9], updated[10], *updated[:6], *vectors)


def solution(mesh):
    in_specs = (
        P("dp", "sp", None),
        P("dp", "sp", None),
        P("dp", None),
        P("dp", None),
        P(),
        P("dp", None, None),
        P("dp", None, None),
        P("dp", None, None),
        P("dp", None, None),
        P("dp", None, None),
        P("dp", None, None),
        P("dp", None, None),
        P("dp"),
        P("dp"),
        P("dp"),
    )
    out_specs = (
        P("dp", "sp", None),
        P("dp", "sp", None),
        P("dp", None, None),
        P("dp", None, None),
        P("dp", None, None),
        P("dp", None, None),
        P("dp", None, None),
        P("dp", None, None),
        P("dp"),
        P("dp"),
        P("dp"),
    )
    chosen = fast_device if dict(mesh.shape) == {"dp": 8, "sp": 4} else per_device
    return jax.shard_map(
        chosen, mesh=mesh, in_specs=in_specs, out_specs=out_specs, check_vma=False
    )
```

profile of v0, /device:TPU:1, one launch (start us, length us, event | category | flops | bytes accessed | tf_op | source)
XLA Modules:
  0.0 206.1 jit_solution(17820280993468472855)
XLA Ops:
  0.6 0.7 reshape.37.vector
  1.3 63.6 %gather_all.1 = (bf16[48,400,384]{2,1,0:T(8,128)(2,1)}, bf16[4,128,768]{2,1,0:T(8,128)(2,1)}, bf16[4,128,768]{2,1,0:T(8,128)(2,1)}) custom-call(f32[6,384,384]{2,1,0:T(8,128)} %weights.3, f32[1,384]{1,0:T(1,128)S(1)} %reshape.37.vector, bf16[4,128,768]{2,1,0:T(8,128)(2,1)} %tokens.1, bf16[4,128,768]{2,1,0:T(8,128)(2,1)} %grads.1), custom_call_target="tpu_custom_call" | custom-call | tf_op jit(solution)/shard_map/gather_all/pallas_call | solution.py:524
  64.9 52.5 %run_layer.1 = (bf16[48,400,384]{2,1,0:T(8,128)(2,1)}, bf16[512,768]{1,0:T(8,128)(2,1)}, bf16[512,768]{1,0:T(8,128)(2,1)}) custom-call(s32[48]{0:T(128)} %owner.1, bf16[48,400,384]{2,1,0:T(8,128)(2,1)} %get-tuple-element.31.weights, bf16[512,768]{1,0:T(8,128)(2,1)} %bitcast.6, bf16[512,768]{1,0:T(8,128)(2,1)} %bitcast.7, s32[4,512]{1,0:T(4,128)} %segments.1), custom_call_target="tpu_custom_call" | custom-call | tf_op jit(solution)/shard_map/run_layer/pallas_call | solution.py:851
  117.5 0.0 copy-start
  117.5 0.0 copy-start.1
  117.5 0.0 copy-start.2
  117.5 0.0 copy-start.3
  117.5 0.0 copy-start.4
  117.5 0.0 copy-start.5
  117.6 0.0 copy-start.6
  117.6 72.0 %reduce_all.1 = (bf16[6,400,384]{2,1,0:T(8,128)(2,1)S(1)}, bf16[4,128,768]{2,1,0:T(8,128)(2,1)}, bf16[4,128,768]{2,1,0:T(8,128)(2,1)}) custom-call(bf16[48,400,384]{2,1,0:T(8,128)(2,1)} %get-tuple-element.34.grads, bf16[4,128,768]{2,1,0:T(8,128)(2,1)} %bitcast.4, bf16[4,128,768]{2,1,0:T(8,128)(2,1)} %bitcast.5), custom_call_target="tpu_custom_call" | custom-call | tf_op jit(solution)/shard_map/reduce_all/pallas_call | solution.py:1157
  189.5 0.0 copy-done
  189.6 0.0 copy-done.1
  189.6 0.0 copy-done.2
  189.6 0.0 copy-done.3
  189.6 0.0 copy-done.4
  189.6 0.0 copy-done.5
  189.6 0.0 copy-done.6
  189.6 16.3 %update_all.1 = (f32[6,384,384]{2,1,0:T(8,128)}, f32[6,384,384]{2,1,0:T(8,128)}, f32[6,384,384]{2,1,0:T(8,128)}, f32[6,384,384]{2,1,0:T(8,128)}, f32[6,384,384]{...) custom-call(bf16[6,400,384]{2,1,0:T(8,128)(2,1)S(1)} %get-tuple-elem, ...), custom_call_target="tpu_custom_call" | custom-call | tf_op jit(solution)/shard_map/update_all/pallas_call | solution.py:1282
Async XLA Ops:
  117.5 72.1 %copy-start = (f32[6,384,384]{2,1,0:T(8,128)S(1)}, f32[6,384,384]{2,1,0:T(8,128)}, u32[]{:S(2)}) copy-start(f32[6,384,384]{2,1,0:T(8,128)} %weights.3) | copy-start | bytes 10616836
  117.5 72.1 %copy-start.1 = (f32[6,384,384]{2,1,0:T(8,128)S(1)}, f32[6,384,384]{2,1,0:T(8,128)}, u32[]{:S(2)}) copy-start(f32[6,384,384]{2,1,0:T(8,128)} %first.1) | copy-start | bytes 10616836
  117.5 72.1 %copy-start.2 = (f32[6,384,384]{2,1,0:T(8,128)S(1)}, f32[6,384,384]{2,1,0:T(8,128)}, u32[]{:S(2)}) copy-start(f32[6,384,384]{2,1,0:T(8,128)} %second.1) | copy-start | bytes 10616836
  117.5 72.1 %copy-start.3 = (f32[6,384,384]{2,1,0:T(8,128)S(1)}, f32[6,384,384]{2,1,0:T(8,128)}, u32[]{:S(2)}) copy-start(f32[6,384,384]{2,1,0:T(8,128)} %left_rot.1) | copy-start | bytes 10616836
  117.5 72.0 %copy-start.4 = (f32[384]{0:T(512)S(1)}, f32[384]{0:T(512)}, u32[]{:S(2)}) copy-start(f32[384]{0:T(512)} %vec.1) | copy-start | bytes 4612
  117.5 72.0 %copy-start.5 = (f32[384]{0:T(512)S(1)}, f32[384]{0:T(512)}, u32[]{:S(2)}) copy-start(f32[384]{0:T(512)} %vec_first.1) | copy-start | bytes 4612
  117.6 72.0 %copy-start.6 = (f32[384]{0:T(512)S(1)}, f32[384]{0:T(512)}, u32[]{:S(2)}) copy-start(f32[384]{0:T(512)} %vec_second.1) | copy-start | bytes 4612
where the time goes:
time: 206 us
  Pallas kernels  204 us (99%)
    pallas_call x1, Pallas kernels, reduce_all(): pl.pallas_call(reduce_kernel, name='reduce_all', out_shape=[jax.ShapeDtyp...  72 us
    pallas_call x1, Pallas kernels, gather_all(): pl.pallas_call(gather_kernel, name='gather_all', out_shape=[pltpu.HBM((48...  63.6 us
    pallas_call x1, Pallas kernels, run_layer(): pl.pallas_call(layer_kernel, name='run_layer', out_shape=[jax.ShapeDtypeS...  52.5 us
    pallas_call x1, Pallas kernels, update_all(): pl.pallas_call(update_kernel, name='update_all', out_shape=[matrix] * 5 +...  16.3 us

commit v1 on v0

--- a/solution.py
+++ b/solution.py
@@ -380,7 +380,7 @@
     return ref.at[slot, pl.ds(pl.multiple_of(row, height), height)]
 
 
-def gather_kernel(weights, vector, tokens, grads, out, token_row, grad_row, wide, narrow, *sems):
+def gather_kernel(weights, vector, tokens, grads, out, token_row, grad_row, wide, narrow, gain_row, *sems):
     z, y, x, c = place()
     dp = z * 2 + y
     sp = x * 2 + c
@@ -393,6 +393,9 @@
         "up": (dp + 2, sp), "down": (dp - 2, sp), "y": (z * 2 + 1 - y, sp),
         "x": (dp, (1 - x) * 2 + c), "mate": (dp, x * 2 + 1 - c), "pass": (dp, x * 2 + 1 - c),
     }
+    take_gains = pltpu.make_async_copy(vector, gain_row, load_sem.at[6])
+    take_gains.start()
+
     def load_of(i):
         return pltpu.make_async_copy(weights.at[i], wide.at[i], load_sem.at[i])
 
@@ -404,8 +407,9 @@
     ]
     for keep in keeps:
         keep.start()
-    gains = jnp.broadcast_to(vector[...], (16, BLK)).astype(jnp.bfloat16)
     greet(z, y, x, c)
+    take_gains.wait()
+    gains = jnp.broadcast_to(gain_row[...].reshape(1, BLK), (16, BLK)).astype(jnp.bfloat16)
 
     def row_copy(which, source, landing, step, arrival):
         peer = (sp + step) % 4
@@ -529,18 +533,19 @@
             pltpu.HBM(tokens.shape, jnp.bfloat16),
             pltpu.HBM(grads.shape, jnp.bfloat16),
         ],
-        in_specs=[anywhere, pl.BlockSpec(memory_space=pltpu.VMEM), anywhere, anywhere],
-        out_specs=[anywhere, anywhere, anywhere],
+        in_specs=[anywhere] * 4,
+        out_specs=[anywhere] * 3,
         scratch_shapes=[
             pltpu.VMEM((6, BLK, BLK), jnp.float32),
             pltpu.VMEM((6, PITCH, BLK), jnp.bfloat16),
-            dma((6,)), dma((6,)), dma((2, 3)), dma((2, 4)), dma((2,)),
+            pltpu.VMEM((BLK,), jnp.float32),
+            dma((7,)), dma((6,)), dma((2, 3)), dma((2, 4)), dma((2,)),
         ]
         + [dma((8,))] * flows,
         compiler_params=pltpu.CompilerParams(
             collective_id=0, has_side_effects=True, vmem_limit_bytes=24 << 20
         ),
-    )(in_hbm(weights), vector.reshape(1, BLK), in_hbm(tokens), in_hbm(grads))
+    )(in_hbm(weights), in_hbm(vector), in_hbm(tokens), in_hbm(grads))
 
 
 ROW = 512

time: 206 us -> 206 us (level)
  no operation moved by 1% of the time
where the time goes in v1:
time: 206 us; the launch traced here: 205 us
  Pallas kernels  204 us (99%)
    pallas_call x1, Pallas kernels, reduce_all(): pl.pallas_call(reduce_kernel, name='reduce_all', out_shape=[jax.ShapeDtyp...  72 us
    pallas_call x1, Pallas kernels, gather_all(): pl.pallas_call(gather_kernel, name='gather_all', out_shape=[pltpu.HBM((48...  63.6 us
    pallas_call x1, Pallas kernels, run_layer(): pl.pallas_call(layer_kernel, name='run_layer', out_shape=[jax.ShapeDtypeS...  52.5 us
    pallas_call x1, Pallas kernels, update_all(): pl.pallas_call(update_kernel, name='update_all', out_shape=[matrix] * 5 +...  16.3 us

profile of v1, /device:TPU:1, one launch (start us, length us, event | category | flops | bytes accessed | tf_op | source)
XLA Modules:
  0.0 205.4 jit_solution(17113168601968271200)
XLA Ops:
  0.6 63.6 %gather_all.1 = (bf16[48,400,384]{2,1,0:T(8,128)(2,1)}, bf16[4,128,768]{2,1,0:T(8,128)(2,1)}, bf16[4,128,768]{2,1,0:T(8,128)(2,1)}) custom-call(f32[6,384,384]{2,1,0:T(8,128)} %weights.3, f32[384]{0:T(512)} %vec.1, bf16[4,128,768]{2,1,0:T(8,128)(2,1)} %tokens.1, bf16[4,128,768]{2,1,0:T(8,128)(2,1)} %grads.1), custom_call_target="tpu_custom_call" | custom-call | tf_op jit(solution)/shard_map/gather_all/pallas_call | solution.py:528
  64.3 52.5 %run_layer.1 = (bf16[48,400,384]{2,1,0:T(8,128)(2,1)}, bf16[512,768]{1,0:T(8,128)(2,1)}, bf16[512,768]{1,0:T(8,128)(2,1)}) custom-call(s32[48]{0:T(128)} %owner.1, bf16[48,400,384]{2,1,0:T(8,128)(2,1)} %get-tuple-element.31.weights, bf16[512,768]{1,0:T(8,128)(2,1)} %bitcast.6, bf16[512,768]{1,0:T(8,128)(2,1)} %bitcast.7, s32[4,512]{1,0:T(4,128)} %segments.1), custom_call_target="tpu_custom_call" | custom-call | tf_op jit(solution)/shard_map/run_layer/pallas_call | solution.py:856
  116.8 0.0 copy-start
  116.8 0.0 copy-start.1
  116.8 0.0 copy-start.2
  116.9 0.0 copy-start.3
  116.9 0.0 copy-start.4
  116.9 0.0 copy-start.5
  116.9 0.0 copy-start.6
  116.9 72.0 %reduce_all.1 = (bf16[6,400,384]{2,1,0:T(8,128)(2,1)S(1)}, bf16[4,128,768]{2,1,0:T(8,128)(2,1)}, bf16[4,128,768]{2,1,0:T(8,128)(2,1)}) custom-call(bf16[48,400,384]{2,1,0:T(8,128)(2,1)} %get-tuple-element.34.grads, bf16[4,128,768]{2,1,0:T(8,128)(2,1)} %bitcast.4, bf16[4,128,768]{2,1,0:T(8,128)(2,1)} %bitcast.5), custom_call_target="tpu_custom_call" | custom-call | tf_op jit(solution)/shard_map/reduce_all/pallas_call | solution.py:1162
  188.9 0.0 copy-done
  188.9 0.0 copy-done.1
  188.9 0.0 copy-done.2
  188.9 0.0 copy-done.3
  188.9 0.0 copy-done.4
  188.9 0.0 copy-done.5
  188.9 0.0 copy-done.6
  189.0 16.3 %update_all.1 = (f32[6,384,384]{2,1,0:T(8,128)}, f32[6,384,384]{2,1,0:T(8,128)}, f32[6,384,384]{2,1,0:T(8,128)}, f32[6,384,384]{2,1,0:T(8,128)}, f32[6,384,384]{...) custom-call(bf16[6,400,384]{2,1,0:T(8,128)(2,1)S(1)} %get-tuple-elem, ...), custom_call_target="tpu_custom_call" | custom-call | tf_op jit(solution)/shard_map/update_all/pallas_call | solution.py:1287
Async XLA Ops:
  116.8 72.1 %copy-start = (f32[6,384,384]{2,1,0:T(8,128)S(1)}, f32[6,384,384]{2,1,0:T(8,128)}, u32[]{:S(2)}) copy-start(f32[6,384,384]{2,1,0:T(8,128)} %weights.3) | copy-start | bytes 10616836
  116.8 72.1 %copy-start.1 = (f32[6,384,384]{2,1,0:T(8,128)S(1)}, f32[6,384,384]{2,1,0:T(8,128)}, u32[]{:S(2)}) copy-start(f32[6,384,384]{2,1,0:T(8,128)} %first.1) | copy-start | bytes 10616836
  116.8 72.1 %copy-start.2 = (f32[6,384,384]{2,1,0:T(8,128)S(1)}, f32[6,384,384]{2,1,0:T(8,128)}, u32[]{:S(2)}) copy-start(f32[6,384,384]{2,1,0:T(8,128)} %second.1) | copy-start | bytes 10616836
  116.9 72.1 %copy-start.3 = (f32[6,384,384]{2,1,0:T(8,128)S(1)}, f32[6,384,384]{2,1,0:T(8,128)}, u32[]{:S(2)}) copy-start(f32[6,384,384]{2,1,0:T(8,128)} %left_rot.1) | copy-start | bytes 10616836
  116.9 72.1 %copy-start.4 = (f32[384]{0:T(512)S(1)}, f32[384]{0:T(512)}, u32[]{:S(2)}) copy-start(f32[384]{0:T(512)} %vec.1) | copy-start | bytes 4612
  116.9 72.1 %copy-start.5 = (f32[384]{0:T(512)S(1)}, f32[384]{0:T(512)}, u32[]{:S(2)}) copy-start(f32[384]{0:T(512)} %vec_first.1) | copy-start | bytes 4612
  116.9 72.1 %copy-start.6 = (f32[384]{0:T(512)S(1)}, f32[384]{0:T(512)}, u32[]{:S(2)}) copy-start(f32[384]{0:T(512)} %vec_second.1) | copy-start | bytes 4612
